TPU v7x, 512 devices: a whole 4x4x16 slice. The times are simulated.
512 devices in a mesh: row: 8 (over x, core), col: 16 (over z), layer: 4 (over y).
Axes of the slice: x: 4, y: 4, z: 16, core: 2. Of those that a mesh axis runs over, the one named last changes fastest.
Arguments:
- occurrences: bfloat16 [8192, 10240], P(('row', 'col', 'layer')), may hold values from -6 to 6
- idf_weight: float32 [8192], P(('row', 'col', 'layer')), may hold values from 0.25 to 2
- pattern: int32 [64, 80], replicated, may hold values 0 or 1
Outputs:
- margin: bfloat16 [10240, 10240], P('row', 'col')
All inputs are finite; a program needn't handle non-finite values.
Results may differ from a plain program's by a relative error of at most 0.0058.
Values may be sent and summed in bfloat16 or wider, within the bound.
No kernel may reach another device: no remote copies, remote signals or barrier semaphores. Data moves between devices by JAX's collectives and lax.ppermute only.
A program may use at most 64 MiB of HBM per device.

v0:
```python
import math
import jax
import jax.numpy as jnp
from jax import lax
from jax.sharding import PartitionSpec as P


def finish(partial_rows, row_start, col_start, factor):
    row_ids = row_start + lax.broadcasted_iota(jnp.int32, partial_rows.shape, 0)
    col_ids = col_start + lax.broadcasted_iota(jnp.int32, partial_rows.shape, 1)
    result = jnp.where(row_ids == col_ids, jnp.float32(0.0), partial_rows * factor)
    return result.astype(jnp.bfloat16)


def body(occurrences, idf_weight, pattern):
    owned, reads = occurrences.shape
    n_rows = lax.axis_size("row")
    n_cols = lax.axis_size("col")
    n_layers = lax.axis_size("layer")
    factor = 1.0 / math.sqrt(owned * n_rows * n_cols * n_layers)
    owner = lax.axis_index(("row", "col", "layer"))
    block_row = owner * owned // 128
    flags = lax.dynamic_slice_in_dim(pattern, block_row, 1, 0)[0]
    read_mask = jnp.repeat(flags.astype(jnp.float32), 128)
    weighted = (occurrences.astype(jnp.float32) * idf_weight[:, None] * read_mask[None, :]).astype(
        jnp.bfloat16
    )
    piece_len = reads // (n_rows * n_cols)
    reordered = (
        weighted.reshape(owned, n_cols, n_rows, piece_len)
        .transpose(0, 2, 1, 3)
        .reshape(owned, reads)
    )
    row_part, col_part = (
        lax.all_to_all(weighted, ("row", "col"), split_axis=1, concat_axis=0, tiled=True),
        lax.all_to_all(reordered, ("row", "col"), split_axis=1, concat_axis=0, tiled=True),
    )
    column_reads = lax.all_gather(col_part, "row", axis=1, tiled=True)
    partial_tile = lax.dot_general(
        lax.all_gather(row_part, "col", axis=1, tiled=True),
        column_reads,
        (((0,), (0,)), ((), ())),
        preferred_element_type=jnp.float32,
    )
    row_count = partial_tile.shape[0]
    row_start = lax.axis_index("row") * row_count
    col_start = lax.axis_index("col") * partial_tile.shape[1]
    total = lax.psum(partial_tile, "layer")
    return finish(total, row_start, col_start, factor)


def solution(mesh):
    placed = (P(("row", "col", "layer"), None), P(("row", "col", "layer")), P())
    return jax.shard_map(
        body, mesh=mesh, in_specs=placed, out_specs=P("row", "col"), check_vma=False
    )
```

profile of v0, /device:TPU:1, one launch (start us, length us, event | category | flops | bytes accessed | tf_op | source)
XLA Modules:
  0.0 287.5 jit_solution(10885676402827663510)
XLA Ops:
  6.5 0.0 all-gather.5.cloned.1.call-start
  6.5 0.7 convert_bitcast_fusion
  7.2 0.1 broadcast_bitcast_fusion
  7.3 1.1 multiply_convert_fusion
  8.4 0.6 reshape.14
  9.1 0.1 copy.9
  9.2 0.3 copy.10
  9.6 52.5 %all_to_all.38 = bf16[16,128,80]{2,0,1:T(8,128)(2,1)S(1)} all-to-all(bf16[16,128,80]{2,0,1:T(8,128)(2,1)S(1)} %copy.10), channel_id=1, replica_groups=mesh['row'=8,'col'=16,'layer'=4] {'row','col'}, dimensions={1} | all-to-all | bytes 655360 | tf_op jit(solution)/shard_map/all_to_all | solution.py:36
  62.0 0.9 copy.11
  63.0 0.0 all-gather.5.cloned.1.call-update
  63.0 0.0 all-gather.3.cloned.1.call-start
  63.0 0.6 all_to_all.28
  63.7 0.3 copy.7
  64.0 39.7 %all_to_all.39 = bf16[16,128,80]{2,0,1:T(8,128)(2,1)S(1)} all-to-all(bf16[16,128,80]{2,0,1:T(8,128)(2,1)S(1)} %copy.7), channel_id=1, replica_groups=mesh['row'=8,'col'=16,'layer'=4] {'row','col'}, dimensions={1} | all-to-all | bytes 655360 | tf_op jit(solution)/shard_map/all_to_all | solution.py:35
  103.8 0.9 copy.8
  104.7 0.0 all-gather.3.cloned.1.call-update
  104.7 0.0 all-reduce.2.cloned.1.call-start
  104.8 0.0 all-gather.5.cloned.1.call-done
  104.8 67.3 %all-gather.3.cloned.1.call-done = bf16[2048,1280]{0,1:T(8,128)(2,1)} async-done(((bf16[2048,80]{0,1:T(8,128)(2,1)}), bf16[2048,1280]{0,1:T(8,128)(2,1)}) %all-gather.3.cloned.1.call-update) | async-done | bytes 5242896 | tf_op jit(solution)/shard_map/all_gather | solution.py:40
  172.1 9.3 %fusion = f32[1280,640]{1,0:T(8,128)} fusion(bf16[2048,1280]{0,1:T(8,128)(2,1)} %all-gather.3.cloned.1.call-done, bf16[2048,640]{0,1:T(8,128)(2,1)} %all-gather.5.cloned.1.call-done), kind=kOutput, calls=%fused_computation.6 | convolution fusion | flops 3355443200 | bytes 11141120 | tf_op jit(solution)/shard_map/dot_general | solution.py:39
  181.3 0.0 all-reduce.2.cloned.1.call-update
  181.4 96.0 %all-reduce.2.cloned.1.call-done = f32[1280,640]{1,0:T(8,128)} async-done(((f32[1280,640]{1,0:T(8,128)}), f32[1280,640]{1,0:T(8,128)}) %all-reduce.2.cloned.1.call-update) | async-done | bytes 3276816 | tf_op jit(solution)/shard_map/psum | solution.py:48
  277.4 3.5 %select_convert_fusion = bf16[1280,640]{1,0:T(8,128)(2,1)} fusion(f32[1280,640]{1,0:T(8,128)} %all-reduce.2.cloned.1.call-done, s32[640]{0:T(1024)S(1)} %iota_add_fusion.1, s32[1280]{0:T(1024)S(1)} %iota_add_fusion), kind=kLoop, calls=%fused_computation | loop fusion | flops 3276800 | bytes 4922880 | tf_op jit(solution)/shard_map/convert_element_type | solution.py:12
  (2 shorter events, 0.0 us)
Async XLA Ops:
  6.5 98.3 %all-gather.5.cloned.1.call-start = ((), (), s32[]{:S(2)}) async-start(), calls=%async_computation.3 | async-start | bytes 2949120 | tf_op jit(solution)/shard_map/all_gather | solution.py:38
  63.0 109.1 %all-gather.3.cloned.1.call-start = ((), (), s32[]{:S(2)}) async-start(), calls=%async_computation.2 | async-start | bytes 5570560 | tf_op jit(solution)/shard_map/all_gather | solution.py:40
  104.7 172.7 %all-reduce.2.cloned.1.call-start = ((), (), s32[]{:S(2)}) async-start(), calls=%async_computation.4 | async-start | bytes 6553600 | tf_op jit(solution)/shard_map/psum | solution.py:48
Sparse Core Ops, SparseCore 0:
  63.1 29.0 all-gather.4
  104.9 67.1 all-gather.2
  181.5 95.8 all-reduce.1
where the time goes:
time: 288 us; the launch traced here: 287 us
  waiting for transfers between devices  163 us (57%)
  blocking collectives  92.2 us (32%)
  between operations  13.2 us (5%)
  matrix products  9.28 us (3%)
  other arithmetic  5.36 us (2%)
  local copies, waits for them, and re-layouts  4.02 us (1%)
    psum x1, waiting for transfers between devices, body(): total = lax.psum(partial_tile, 'layer')  96 us
    all_gather x1, waiting for transfers between devices, body(): lax.all_gather(row_part, 'col', axis=1, tiled=True)  67.3 us
    all_to_all x1, blocking collectives, body(): lax.all_to_all(reordered, ('row', 'col'), split_axis=1, concat_axis=0, ti...  52.5 us
    all_to_all x1, blocking collectives, body(): lax.all_to_all(weighted, ('row', 'col'), split_axis=1, concat_axis=0, til...  39.7 us
    dot_general x1, matrix products, body(): lax.dot_general(lax.all_gather(row_part, 'col', axis=1, tiled=True), colu...  9.28 us
  transfers between devices with their start and end apart: 3, of which 2 were waited for; matrix products, arithmetic and copies ran while one was open for 0% of the time, Pallas kernels for 0%

commit v1 on v0

--- a/solution.py
+++ b/solution.py
@@ -3,6 +3,24 @@
 import jax.numpy as jnp
 from jax import lax
 from jax.sharding import PartitionSpec as P
+
+
+def gather_around(value, axis, dim):
+    ways, here, lap = (lax.axis_size(axis), lax.axis_index(axis), value.shape[dim])
+    lengths = [n * ways if d == dim else n for d, n in enumerate(value.shape)]
+    full = lax.dynamic_update_slice_in_dim(
+        jnp.zeros(lengths, value.dtype), value, here * lap, axis=dim
+    )
+    going_up = going_down = value
+    for far in range(1, ways // 2 + 1):
+        going_up = lax.ppermute(going_up, axis, [(d, (d + 1) % ways) for d in range(ways)])
+        full = lax.dynamic_update_slice_in_dim(full, going_up, (here - far) % ways * lap, axis=dim)
+        if 2 * far < ways:
+            going_down = lax.ppermute(going_down, axis, [(d, (d - 1) % ways) for d in range(ways)])
+            full = lax.dynamic_update_slice_in_dim(
+                full, going_down, (here + far) % ways * lap, axis=dim
+            )
+    return full
 
 
 def finish(partial_rows, row_start, col_start, factor):
@@ -37,7 +55,7 @@
     )
     column_reads = lax.all_gather(col_part, "row", axis=1, tiled=True)
     partial_tile = lax.dot_general(
-        lax.all_gather(row_part, "col", axis=1, tiled=True),
+        gather_around(row_part, "col", 1),
         column_reads,
         (((0,), (0,)), ((), ())),
         preferred_element_type=jnp.float32,

time: 288 us -> 429 us (1.49)
  local copies, waits for them, and re-layouts: 4.02 us -> 109 us
  starting transfers between devices: 0.09 us -> 47.3 us
  waiting for transfers between devices: 163 us -> 149 us
    dynamic_update_slice x0 -> x16, local copies, waits for them, and re-layouts: none -> 103 us  [the longest x8 51.3 us: gather_around(): lax.dynamic_update_slice_in_dim(full, going_up, (here - far) % ways * lap...]
    all_gather x1 -> x0, waiting for transfers between devices: 67.3 us -> none  [body(): lax.all_gather(row_part, 'col', axis=1, tiled=True)]
    ppermute x0 -> x15, waiting for transfers between devices: none -> 52.4 us  [the longest x8 52.4 us: gather_around(): lax.ppermute(going_up, axis, [(d, (d + 1) % ways) for d in range(ways)])]
    ppermute x0 -> x15, starting transfers between devices: none -> 47.3 us  [the longest x7 28 us: gather_around(): lax.ppermute(going_down, axis, [(d, (d - 1) % ways) for d in range(ways)])]
  transfers between devices with their start and end apart: 3 -> 17, of which waited for: 2 -> 8; matrix products, arithmetic and copies ran while one was open for 0% -> 25% of each run, Pallas kernels for 0% -> 0%
where the time goes in v1:
time: 429 us; the launch traced here: 426 us
  waiting for transfers between devices  149 us (35%)
  local copies, waits for them, and re-layouts  109 us (25%)
  blocking collectives  92.2 us (21%)
  starting transfers between devices  47.3 us (11%)
  between operations  14 us (3%)
  matrix products  9.33 us (2%)
  other arithmetic  5.36 us (1%)
    psum x1, waiting for transfers between devices, body(): total = lax.psum(partial_tile, 'layer')  96.1 us
    all_to_all x1, blocking collectives, body(): lax.all_to_all(reordered, ('row', 'col'), split_axis=1, concat_axis=0, ti...  52.5 us
    ppermute x8, waiting for transfers between devices, gather_around(): lax.ppermute(going_up, axis, [(d, (d + 1) % ways) for d in range(ways)])  52.4 us
    dynamic_update_slice x8, local copies, waits for them, and re-layouts, gather_around(): lax.dynamic_update_slice_in_dim(full, going_up, (here - far) % ways * lap...  51.3 us
    dynamic_update_slice x7, local copies, waits for them, and re-layouts, gather_around(): lax.dynamic_update_slice_in_dim(full, going_down, (here + far) % ways * l...  46.3 us
    all_to_all x1, blocking collectives, body(): lax.all_to_all(weighted, ('row', 'col'), split_axis=1, concat_axis=0, til...  39.7 us
    ppermute x7, starting transfers between devices, gather_around(): lax.ppermute(going_down, axis, [(d, (d - 1) % ways) for d in range(ways)])  28 us
    ppermute x8, starting transfers between devices, gather_around(): lax.ppermute(going_up, axis, [(d, (d + 1) % ways) for d in range(ways)])  19.3 us
  transfers between devices with their start and end apart: 17, of which 8 were waited for; matrix products, arithmetic and copies ran while one was open for 25% of the time, Pallas kernels for 0%

profile of v1, /device:TPU:1, one launch (start us, length us, event | category | flops | bytes accessed | tf_op | source)
XLA Modules:
  0.0 425.8 jit_solution(7443391282822093595)
XLA Ops:
  6.5 0.7 convert_bitcast_fusion
  7.2 0.1 broadcast_bitcast_fusion
  7.3 1.1 multiply_convert_fusion
  8.4 0.6 reshape.14
  9.1 0.1 copy.8
  9.2 0.3 copy.9
  9.6 52.5 %all_to_all.38 = bf16[16,128,80]{2,0,1:T(8,128)(2,1)S(1)} all-to-all(bf16[16,128,80]{2,0,1:T(8,128)(2,1)S(1)} %copy.9), channel_id=1, replica_groups=mesh['row'=8,'col'=16,'layer'=4] {'row','col'}, dimensions={1} | all-to-all | bytes 655360 | tf_op jit(solution)/shard_map/all_to_all | solution.py:54
  62.0 0.9 copy.10
  63.0 0.0 all-gather.2.cloned.1.call-update
  63.0 0.0 all-reduce.2.cloned.1.call-start
  63.0 0.6 all_to_all.28
  63.7 0.3 copy.7
  64.0 39.7 %all_to_all.39 = bf16[16,128,80]{2,0,1:T(8,128)(2,1)S(1)} all-to-all(bf16[16,128,80]{2,0,1:T(8,128)(2,1)S(1)} %copy.7), channel_id=1, replica_groups=mesh['row'=8,'col'=16,'layer'=4] {'row','col'}, dimensions={1} | all-to-all | bytes 655360 | tf_op jit(solution)/shard_map/all_to_all | solution.py:53
  103.8 4.1 collective-permute-start
  107.9 2.3 collective-permute-start.1
  110.3 10.2 %collective-permute-done = bf16[2048,80]{1,0:T(8,128)(2,1)S(1)} collective-permute-done((bf16[2048,80]{1,0:T(8,128)(2,1)S(1)}, bf16[2048,80]{1,0:T(8,128)(2,1)S(1)}, u32[]{:S(2)}, u32[]{:S(2)}) %collective-permute-start) | collective-permute-done | bytes 327712 | tf_op jit(solution)/shard_map/ppermute | solution.py:16
  120.5 3.2 collective-permute-start.2
  123.7 0.0 collective-permute-done.1
  123.8 3.3 collective-permute-start.3
  127.0 9.3 %collective-permute-done.2 = bf16[2048,80]{1,0:T(8,128)(2,1)S(1)} collective-permute-done((bf16[2048,80]{1,0:T(8,128)(2,1)S(1)}, bf16[2048,80]{1,0:T(8,128)(2,1)S(1)}, u32[]{:S(2)}, u32[]{:S(2)}) %collective-permute-start.2) | collective-permute-done | bytes 327712 | tf_op jit(solution)/shard_map/ppermute | solution.py:16
  136.4 2.4 collective-permute-start.4
  138.8 0.0 collective-permute-done.3
  138.8 4.1 collective-permute-start.5
  142.9 8.4 %collective-permute-done.4 = bf16[2048,80]{1,0:T(8,128)(2,1)S(1)} collective-permute-done((bf16[2048,80]{1,0:T(8,128)(2,1)S(1)}, bf16[2048,80]{1,0:T(8,128)(2,1)S(1)}, u32[]{:S(2)}, u32[]{:S(2)}) %collective-permute-start.4) | collective-permute-done | bytes 327712 | tf_op jit(solution)/shard_map/ppermute | solution.py:16
  151.3 1.9 collective-permute-start.6
  153.2 0.0 collective-permute-done.5
  153.2 0.0 copy-start
  153.3 4.6 %collective-permute-start.7 = (bf16[2048,80]{1,0:T(8,128)(2,1)S(1)}, bf16[2048,80]{1,0:T(8,128)(2,1)S(1)}, u32[]{:S(2)}, u32[]{:S(2)}) collective-permute-start(bf16[2048,80]{1,0:T(8,128)(2,1)S(1)} %collective-permute-done.5), channel_id=1, source_target_pairs={{0,60},{4,0},{8,4},{12,8},{16,12},{20,16},{24,20},{28,24},{32,28},... | collective-permute-start | bytes 983048 | tf_op jit(solution)/shard_map/ppermute | solution.py:19
  157.8 7.5 %collective-permute-done.6 = bf16[2048,80]{1,0:T(8,128)(2,1)S(1)} collective-permute-done((bf16[2048,80]{1,0:T(8,128)(2,1)S(1)}, bf16[2048,80]{1,0:T(8,128)(2,1)S(1)}, u32[]{:S(2)}, u32[]{:S(2)}) %collective-permute-start.6) | collective-permute-done | bytes 327712 | tf_op jit(solution)/shard_map/ppermute | solution.py:16
  165.3 1.9 collective-permute-start.8
  167.2 0.0 collective-permute-done.7
  167.3 4.6 %collective-permute-start.9 = (bf16[2048,80]{1,0:T(8,128)(2,1)S(1)}, bf16[2048,80]{1,0:T(8,128)(2,1)S(1)}, u32[]{:S(2)}, u32[]{:S(2)}) collective-permute-start(bf16[2048,80]{1,0:T(8,128)(2,1)S(1)} %collective-permute-done.7), channel_id=1, source_target_pairs={{0,60},{4,0},{8,4},{12,8},{16,12},{20,16},{24,20},{28,24},{32,28},... | collective-permute-start | bytes 983048 | tf_op jit(solution)/shard_map/ppermute | solution.py:19
  171.9 6.6 %collective-permute-done.8 = bf16[2048,80]{1,0:T(8,128)(2,1)S(1)} collective-permute-done((bf16[2048,80]{1,0:T(8,128)(2,1)S(1)}, bf16[2048,80]{1,0:T(8,128)(2,1)S(1)}, u32[]{:S(2)}, u32[]{:S(2)}) %collective-permute-start.8) | collective-permute-done | bytes 327712 | tf_op jit(solution)/shard_map/ppermute | solution.py:16
  178.4 1.9 collective-permute-start.10
  180.3 0.0 collective-permute-done.9
  180.4 4.6 %collective-permute-start.11 = (bf16[2048,80]{1,0:T(8,128)(2,1)S(1)}, bf16[2048,80]{1,0:T(8,128)(2,1)}, u32[]{:S(2)}, u32[]{:S(2)}) collective-permute-start(bf16[2048,80]{1,0:T(8,128)(2,1)S(1)} %collective-permute-done.9), channel_id=1, source_target_pairs={{0,60},{4,0},{8,4},{12,8},{16,12},{20,16},{24,20},{28,24},{32,28},... | collective-permute-start | bytes 983048 | tf_op jit(solution)/shard_map/ppermute | solution.py:19
  185.0 5.6 %collective-permute-done.10 = bf16[2048,80]{1,0:T(8,128)(2,1)S(1)} collective-permute-done((bf16[2048,80]{1,0:T(8,128)(2,1)S(1)}, bf16[2048,80]{1,0:T(8,128)(2,1)S(1)}, u32[]{:S(2)}, u32[]{:S(2)}) %collective-permute-start.10) | collective-permute-done | bytes 327712 | tf_op jit(solution)/shard_map/ppermute | solution.py:16
  190.6 1.9 collective-permute-start.12
  192.5 0.0 collective-permute-done.11
  192.5 4.6 %collective-permute-start.13 = (bf16[2048,80]{1,0:T(8,128)(2,1)}, bf16[2048,80]{1,0:T(8,128)(2,1)}, u32[]{:S(2)}, u32[]{:S(2)}) collective-permute-start(bf16[2048,80]{1,0:T(8,128)(2,1)} %collective-permute-done.11), channel_id=1, source_target_pairs={{0,60},{4,0},{8,4},{12,8},{16,12},{20,16},{24,20},{28,24},{32,28},... | collective-permute-start | bytes 983048 | tf_op jit(solution)/shard_map/ppermute | solution.py:19
  197.1 4.7 %collective-permute-done.12 = bf16[2048,80]{1,0:T(8,128)(2,1)} collective-permute-done((bf16[2048,80]{1,0:T(8,128)(2,1)S(1)}, bf16[2048,80]{1,0:T(8,128)(2,1)}, u32[]{:S(2)}, u32[]{:S(2)}) %collective-permute-start.12) | collective-permute-done | bytes 327712 | tf_op jit(solution)/shard_map/ppermute | solution.py:16
  201.8 1.9 collective-permute-start.14
  204.1 2.6 broadcast_in_dim.12
  206.7 5.7 %dynamic_update_slice.48 = bf16[2048,1280]{1,0:T(8,128)(2,1)} dynamic-update-slice(bf16[2048,1280]{1,0:T(8,128)(2,1)} %broadcast_in_dim.12, bf16[2048,80]{1,0:T(8,128)(2,1)S(1)} %bitcast.17, s32[]{:T(128)} %constant.124.clone.1, s32[]{:T(128)S(6)} %select_n.124) | dynamic-update-slice | bytes 655364 | tf_op jit(solution)/shard_map/dynamic_update_slice | solution.py:11
  212.3 5.9 %dynamic_update_slice.49 = bf16[2048,1280]{1,0:T(8,128)(2,1)} dynamic-update-slice(bf16[2048,1280]{1,0:T(8,128)(2,1)} %dynamic_update_slice.48, bf16[2048,80]{1,0:T(8,128)(2,1)S(1)} %collective-permute-done, s32[]{:T(128)} %constant.124.clone.1, s32[]{:T(128)S(6)} %select_n.126) | dynamic-update-slice | bytes 655364 | tf_op jit(solution)/shard_map/dynamic_update_slice | solution.py:17
  218.2 6.5 %dynamic_update_slice.50 = bf16[2048,1280]{1,0:T(8,128)(2,1)} dynamic-update-slice(bf16[2048,1280]{1,0:T(8,128)(2,1)} %dynamic_update_slice.49, bf16[2048,80]{1,0:T(8,128)(2,1)S(1)} %collective-permute-done.1, s32[]{:T(128)} %constant.124.clone.1, s32[]{:T(128)S(6)} %select_n.128) | dynamic-update-slice | bytes 655364 | tf_op jit(solution)/shard_map/dynamic_update_slice | solution.py:20
  224.8 6.5 %dynamic_update_slice.51 = bf16[2048,1280]{1,0:T(8,128)(2,1)} dynamic-update-slice(bf16[2048,1280]{1,0:T(8,128)(2,1)} %dynamic_update_slice.50, bf16[2048,80]{1,0:T(8,128)(2,1)S(1)} %collective-permute-done.2, s32[]{:T(128)} %constant.124.clone.1, s32[]{:T(128)S(6)} %select_n.130) | dynamic-update-slice | bytes 655364 | tf_op jit(solution)/shard_map/dynamic_update_slice | solution.py:17
  231.3 6.6 %dynamic_update_slice.52 = bf16[2048,1280]{1,0:T(8,128)(2,1)} dynamic-update-slice(bf16[2048,1280]{1,0:T(8,128)(2,1)} %dynamic_update_slice.51, bf16[2048,80]{1,0:T(8,128)(2,1)S(1)} %collective-permute-done.3, s32[]{:T(128)} %constant.124.clone.1, s32[]{:T(128)S(6)} %select_n.132) | dynamic-update-slice | bytes 655364 | tf_op jit(solution)/shard_map/dynamic_update_slice | solution.py:20
  237.9 6.5 %dynamic_update_slice.53 = bf16[2048,1280]{1,0:T(8,128)(2,1)} dynamic-update-slice(bf16[2048,1280]{1,0:T(8,128)(2,1)} %dynamic_update_slice.52, bf16[2048,80]{1,0:T(8,128)(2,1)S(1)} %collective-permute-done.4, s32[]{:T(128)} %constant.124.clone.1, s32[]{:T(128)S(6)} %select_n.134) | dynamic-update-slice | bytes 655364 | tf_op jit(solution)/shard_map/dynamic_update_slice | solution.py:17
  244.4 6.6 %dynamic_update_slice.54 = bf16[2048,1280]{1,0:T(8,128)(2,1)} dynamic-update-slice(bf16[2048,1280]{1,0:T(8,128)(2,1)} %dynamic_update_slice.53, bf16[2048,80]{1,0:T(8,128)(2,1)S(1)} %copy-done.1, s32[]{:T(128)} %constant.124.clone.1, s32[]{:T(128)S(6)} %select_n.136) | dynamic-update-slice | bytes 655364 | tf_op jit(solution)/shard_map/dynamic_update_slice | solution.py:20
  250.9 6.5 %dynamic_update_slice.55 = bf16[2048,1280]{1,0:T(8,128)(2,1)} dynamic-update-slice(bf16[2048,1280]{1,0:T(8,128)(2,1)} %dynamic_update_slice.54, bf16[2048,80]{1,0:T(8,128)(2,1)S(1)} %copy-done.3, s32[]{:T(128)} %constant.124.clone.1, s32[]{:T(128)S(6)} %select_n.138) | dynamic-update-slice | bytes 655364 | tf_op jit(solution)/shard_map/dynamic_update_slice | solution.py:17
  257.4 6.5 %dynamic_update_slice.56 = bf16[2048,1280]{1,0:T(8,128)(2,1)} dynamic-update-slice(bf16[2048,1280]{1,0:T(8,128)(2,1)} %dynamic_update_slice.55, bf16[2048,80]{1,0:T(8,128)(2,1)S(1)} %copy-done.5, s32[]{:T(128)} %constant.124.clone.1, s32[]{:T(128)S(6)} %select_n.140) | dynamic-update-slice | bytes 655364 | tf_op jit(solution)/shard_map/dynamic_update_slice | solution.py:20
  264.0 6.5 %dynamic_update_slice.57 = bf16[2048,1280]{1,0:T(8,128)(2,1)} dynamic-update-slice(bf16[2048,1280]{1,0:T(8,128)(2,1)} %dynamic_update_slice.56, bf16[2048,80]{1,0:T(8,128)(2,1)S(1)} %copy-done.7, s32[]{:T(128)} %constant.124.clone.1, s32[]{:T(128)S(6)} %select_n.142) | dynamic-update-slice | bytes 655364 | tf_op jit(solution)/shard_map/dynamic_update_slice | solution.py:17
  270.5 6.5 %dynamic_update_slice.58 = bf16[2048,1280]{1,0:T(8,128)(2,1)} dynamic-update-slice(bf16[2048,1280]{1,0:T(8,128)(2,1)} %dynamic_update_slice.57, bf16[2048,80]{1,0:T(8,128)(2,1)S(1)} %copy-done.9, s32[]{:T(128)} %constant.124.clone.1, s32[]{:T(128)S(6)} %select_n.144) | dynamic-update-slice | bytes 655364 | tf_op jit(solution)/shard_map/dynamic_update_slice | solution.py:20
  277.0 6.5 %dynamic_update_slice.59 = bf16[2048,1280]{1,0:T(8,128)(2,1)} dynamic-update-slice(bf16[2048,1280]{1,0:T(8,128)(2,1)} %dynamic_update_slice.58, bf16[2048,80]{1,0:T(8,128)(2,1)S(1)} %copy-done.11, s32[]{:T(128)} %constant.124.clone.1, s32[]{:T(128)S(6)} %select_n.146) | dynamic-update-slice | bytes 655364 | tf_op jit(solution)/shard_map/dynamic_update_slice | solution.py:17
  283.5 6.8 %dynamic_update_slice.60 = bf16[2048,1280]{1,0:T(8,128)(2,1)} dynamic-update-slice(bf16[2048,1280]{1,0:T(8,128)(2,1)} %dynamic_update_slice.59, bf16[2048,80]{1,0:T(8,128)(2,1)} %collective-permute-done.11, s32[]{:T(128)} %constant.124.clone.1, s32[]{:T(128)S(6)} %select_n.148) | dynamic-update-slice | bytes 655364 | tf_op jit(solution)/shard_map/dynamic_update_slice | solution.py:20
  290.3 6.8 %dynamic_update_slice.61 = bf16[2048,1280]{1,0:T(8,128)(2,1)} dynamic-update-slice(bf16[2048,1280]{1,0:T(8,128)(2,1)} %dynamic_update_slice.60, bf16[2048,80]{1,0:T(8,128)(2,1)} %collective-permute-done.12, s32[]{:T(128)} %constant.124.clone.1, s32[]{:T(128)S(6)} %select_n.150) | dynamic-update-slice | bytes 655364 | tf_op jit(solution)/shard_map/dynamic_update_slice | solution.py:17
  297.1 0.0 collective-permute-done.13
  297.1 6.8 %dynamic_update_slice.62 = bf16[2048,1280]{1,0:T(8,128)(2,1)} dynamic-update-slice(bf16[2048,1280]{1,0:T(8,128)(2,1)} %dynamic_update_slice.61, bf16[2048,80]{1,0:T(8,128)(2,1)} %collective-permute-done.13, s32[]{:T(128)} %constant.124.clone.1, s32[]{:T(128)S(6)} %select_n.152) | dynamic-update-slice | bytes 655364 | tf_op jit(solution)/shard_map/dynamic_update_slice | solution.py:20
  304.0 6.0 %dynamic_update_slice.63 = bf16[2048,1280]{1,0:T(8,128)(2,1)} dynamic-update-slice(bf16[2048,1280]{1,0:T(8,128)(2,1)} %dynamic_update_slice.62, bf16[2048,80]{1,0:T(8,128)(2,1)} %collective-permute-done.14, s32[]{:T(128)} %constant.124.clone.1, s32[]{:T(128)S(6)} %select_n.154) | dynamic-update-slice | bytes 655364 | tf_op jit(solution)/shard_map/dynamic_update_slice | solution.py:17
  310.0 9.3 %fusion = f32[1280,640]{1,0:T(8,128)} fusion(bf16[2048,1280]{1,0:T(8,128)(2,1)} %dynamic_update_slice.63, bf16[2048,640]{0,1:T(8,128)(2,1)} %all-gather.2.cloned.1.call-done), kind=kOutput, calls=%fused_computation.6 | convolution fusion | flops 3355443200 | bytes 11141120 | tf_op jit(solution)/shard_map/dot_general | solution.py:57
  319.3 0.0 all-reduce.2.cloned.1.call-update
  319.4 96.1 %all-reduce.2.cloned.1.call-done = f32[1280,640]{1,0:T(8,128)} async-done(((f32[1280,640]{1,0:T(8,128)}), f32[1280,640]{1,0:T(8,128)}) %all-reduce.2.cloned.1.call-update) | async-done | bytes 3276816 | tf_op jit(solution)/shard_map/psum | solution.py:66
  415.5 3.5 select_convert_fusion
  (28 shorter events, 0.1 us)
Async XLA Ops:
  6.5 303.4 %all-gather.2.cloned.1.call-start = ((), (), s32[]{:S(2)}) async-start(), calls=%async_computation.2 | async-start | bytes 2949120 | tf_op jit(solution)/shard_map/all_gather | solution.py:56
  63.0 352.5 %all-reduce.2.cloned.1.call-start = ((), (), s32[]{:S(2)}) async-start(), calls=%async_computation.3 | async-start | bytes 6553600 | tf_op jit(solution)/shard_map/psum | solution.py:66
  103.8 16.7 %collective-permute-start = (bf16[2048,80]{1,0:T(8,128)(2,1)S(1)}, bf16[2048,80]{1,0:T(8,128)(2,1)S(1)}, u32[]{:S(2)}, u32[]{:S(2)}) collective-permute-start(bf16[2048,80]{1,0:T(8,128)(2,1)S(1)} %bitcast.15), channel_id=1, source_target_pairs={{0,4},{4,8},{8,12},{12,16},{16,20},{20,24},{24,28},{28,32},{32,36}... | collective-permute-start | bytes 983048 | tf_op jit(solution)/shard_map/ppermute | solution.py:16
  107.9 15.8 %collective-permute-start.1 = (bf16[2048,80]{1,0:T(8,128)(2,1)S(1)}, bf16[2048,80]{1,0:T(8,128)(2,1)S(1)}, u32[]{:S(2)}, u32[]{:S(2)}) collective-permute-start(bf16[2048,80]{1,0:T(8,128)(2,1)S(1)} %bitcast.16), channel_id=1, source_target_pairs={{0,60},{4,0},{8,4},{12,8},{16,12},{20,16},{24,20},{28,24},{32,28},... | collective-permute-start | bytes 983048 | tf_op jit(solution)/shard_map/ppermute | solution.py:19
  120.5 15.9 %collective-permute-start.2 = (bf16[2048,80]{1,0:T(8,128)(2,1)S(1)}, bf16[2048,80]{1,0:T(8,128)(2,1)S(1)}, u32[]{:S(2)}, u32[]{:S(2)}) collective-permute-start(bf16[2048,80]{1,0:T(8,128)(2,1)S(1)} %collective-permute-done), channel_id=1, source_target_pairs={{0,4},{4,8},{8,12},{12,16},{16,20},{20,24},{24,28},{28,32},{32,36}... | collective-permute-start | bytes 983048 | tf_op jit(solution)/shard_map/ppermute | solution.py:16
  123.8 15.0 %collective-permute-start.3 = (bf16[2048,80]{1,0:T(8,128)(2,1)S(1)}, bf16[2048,80]{1,0:T(8,128)(2,1)S(1)}, u32[]{:S(2)}, u32[]{:S(2)}) collective-permute-start(bf16[2048,80]{1,0:T(8,128)(2,1)S(1)} %collective-permute-done.1), channel_id=1, source_target_pairs={{0,60},{4,0},{8,4},{12,8},{16,12},{20,16},{24,20},{28,24},{32,28},... | collective-permute-start | bytes 983048 | tf_op jit(solution)/shard_map/ppermute | solution.py:19
  136.4 14.9 %collective-permute-start.4 = (bf16[2048,80]{1,0:T(8,128)(2,1)S(1)}, bf16[2048,80]{1,0:T(8,128)(2,1)S(1)}, u32[]{:S(2)}, u32[]{:S(2)}) collective-permute-start(bf16[2048,80]{1,0:T(8,128)(2,1)S(1)} %collective-permute-done.2), channel_id=1, source_target_pairs={{0,4},{4,8},{8,12},{12,16},{16,20},{20,24},{24,28},{28,32},{32,36}... | collective-permute-start | bytes 983048 | tf_op jit(solution)/shard_map/ppermute | solution.py:16
  138.8 14.5 %collective-permute-start.5 = (bf16[2048,80]{1,0:T(8,128)(2,1)S(1)}, bf16[2048,80]{1,0:T(8,128)(2,1)S(1)}, u32[]{:S(2)}, u32[]{:S(2)}) collective-permute-start(bf16[2048,80]{1,0:T(8,128)(2,1)S(1)} %collective-permute-done.3), channel_id=1, source_target_pairs={{0,60},{4,0},{8,4},{12,8},{16,12},{20,16},{24,20},{28,24},{32,28},... | collective-permute-start | bytes 983048 | tf_op jit(solution)/shard_map/ppermute | solution.py:19
  151.3 14.0 %collective-permute-start.6 = (bf16[2048,80]{1,0:T(8,128)(2,1)S(1)}, bf16[2048,80]{1,0:T(8,128)(2,1)S(1)}, u32[]{:S(2)}, u32[]{:S(2)}) collective-permute-start(bf16[2048,80]{1,0:T(8,128)(2,1)S(1)} %collective-permute-done.4), channel_id=1, source_target_pairs={{0,4},{4,8},{8,12},{12,16},{16,20},{20,24},{24,28},{28,32},{32,36}... | collective-permute-start | bytes 983048 | tf_op jit(solution)/shard_map/ppermute | solution.py:16
  153.2 12.1 %copy-start = (bf16[2048,80]{1,0:T(8,128)(2,1)}, bf16[2048,80]{1,0:T(8,128)(2,1)S(1)}, u32[]{:S(2)}) copy-start(bf16[2048,80]{1,0:T(8,128)(2,1)S(1)} %collective-permute-done.5) | copy-start | bytes 983044
  153.3 14.0 %collective-permute-start.7 = (bf16[2048,80]{1,0:T(8,128)(2,1)S(1)}, bf16[2048,80]{1,0:T(8,128)(2,1)S(1)}, u32[]{:S(2)}, u32[]{:S(2)}) collective-permute-start(bf16[2048,80]{1,0:T(8,128)(2,1)S(1)} %collective-permute-done.5), channel_id=1, source_target_pairs={{0,60},{4,0},{8,4},{12,8},{16,12},{20,16},{24,20},{28,24},{32,28},... | collective-permute-start | bytes 983048 | tf_op jit(solution)/shard_map/ppermute | solution.py:19
  165.3 1.9 copy-start.2
  165.3 13.1 %collective-permute-start.8 = (bf16[2048,80]{1,0:T(8,128)(2,1)S(1)}, bf16[2048,80]{1,0:T(8,128)(2,1)S(1)}, u32[]{:S(2)}, u32[]{:S(2)}) collective-permute-start(bf16[2048,80]{1,0:T(8,128)(2,1)S(1)} %collective-permute-done.6), channel_id=1, source_target_pairs={{0,4},{4,8},{8,12},{12,16},{16,20},{20,24},{24,28},{28,32},{32,36}... | collective-permute-start | bytes 983048 | tf_op jit(solution)/shard_map/ppermute | solution.py:16
  167.3 11.2 %copy-start.4 = (bf16[2048,80]{1,0:T(8,128)(2,1)}, bf16[2048,80]{1,0:T(8,128)(2,1)S(1)}, u32[]{:S(2)}) copy-start(bf16[2048,80]{1,0:T(8,128)(2,1)S(1)} %collective-permute-done.7) | copy-start | bytes 983044
  167.3 13.1 %collective-permute-start.9 = (bf16[2048,80]{1,0:T(8,128)(2,1)S(1)}, bf16[2048,80]{1,0:T(8,128)(2,1)S(1)}, u32[]{:S(2)}, u32[]{:S(2)}) collective-permute-start(bf16[2048,80]{1,0:T(8,128)(2,1)S(1)} %collective-permute-done.7), channel_id=1, source_target_pairs={{0,60},{4,0},{8,4},{12,8},{16,12},{20,16},{24,20},{28,24},{32,28},... | collective-permute-start | bytes 983048 | tf_op jit(solution)/shard_map/ppermute | solution.py:19
  178.4 1.9 copy-start.6
  178.4 12.2 %collective-permute-start.10 = (bf16[2048,80]{1,0:T(8,128)(2,1)S(1)}, bf16[2048,80]{1,0:T(8,128)(2,1)S(1)}, u32[]{:S(2)}, u32[]{:S(2)}) collective-permute-start(bf16[2048,80]{1,0:T(8,128)(2,1)S(1)} %collective-permute-done.8), channel_id=1, source_target_pairs={{0,4},{4,8},{8,12},{12,16},{16,20},{20,24},{24,28},{28,32},{32,36}... | collective-permute-start | bytes 983048 | tf_op jit(solution)/shard_map/ppermute | solution.py:16
  180.4 10.2 %copy-start.8 = (bf16[2048,80]{1,0:T(8,128)(2,1)}, bf16[2048,80]{1,0:T(8,128)(2,1)S(1)}, u32[]{:S(2)}) copy-start(bf16[2048,80]{1,0:T(8,128)(2,1)S(1)} %collective-permute-done.9) | copy-start | bytes 983044
  180.4 12.1 %collective-permute-start.11 = (bf16[2048,80]{1,0:T(8,128)(2,1)S(1)}, bf16[2048,80]{1,0:T(8,128)(2,1)}, u32[]{:S(2)}, u32[]{:S(2)}) collective-permute-start(bf16[2048,80]{1,0:T(8,128)(2,1)S(1)} %collective-permute-done.9), channel_id=1, source_target_pairs={{0,60},{4,0},{8,4},{12,8},{16,12},{20,16},{24,20},{28,24},{32,28},... | collective-permute-start | bytes 983048 | tf_op jit(solution)/shard_map/ppermute | solution.py:19
  190.6 1.9 copy-start.10
  190.6 11.2 %collective-permute-start.12 = (bf16[2048,80]{1,0:T(8,128)(2,1)S(1)}, bf16[2048,80]{1,0:T(8,128)(2,1)}, u32[]{:S(2)}, u32[]{:S(2)}) collective-permute-start(bf16[2048,80]{1,0:T(8,128)(2,1)S(1)} %collective-permute-done.10), channel_id=1, source_target_pairs={{0,4},{4,8},{8,12},{12,16},{16,20},{20,24},{24,28},{28,32},{32,36}... | collective-permute-start | bytes 983048 | tf_op jit(solution)/shard_map/ppermute | solution.py:16
  192.5 104.6 %collective-permute-start.13 = (bf16[2048,80]{1,0:T(8,128)(2,1)}, bf16[2048,80]{1,0:T(8,128)(2,1)}, u32[]{:S(2)}, u32[]{:S(2)}) collective-permute-start(bf16[2048,80]{1,0:T(8,128)(2,1)} %collective-permute-done.11), channel_id=1, source_target_pairs={{0,60},{4,0},{8,4},{12,8},{16,12},{20,16},{24,20},{28,24},{32,28},... | collective-permute-start | bytes 983048 | tf_op jit(solution)/shard_map/ppermute | solution.py:19
  201.8 102.1 %collective-permute-start.14 = (bf16[2048,80]{1,0:T(8,128)(2,1)}, bf16[2048,80]{1,0:T(8,128)(2,1)}, u32[]{:S(2)}, u32[]{:S(2)}) collective-permute-start(bf16[2048,80]{1,0:T(8,128)(2,1)} %collective-permute-done.12), channel_id=1, source_target_pairs={{0,4},{4,8},{8,12},{12,16},{16,20},{20,24},{24,28},{28,32},{32,36}... | collective-permute-start | bytes 983048 | tf_op jit(solution)/shard_map/ppermute | solution.py:16
  212.3 32.0 %copy-start.1 = (bf16[2048,80]{1,0:T(8,128)(2,1)S(1)}, bf16[2048,80]{1,0:T(8,128)(2,1)}, u32[]{:S(2)}) copy-start(bf16[2048,80]{1,0:T(8,128)(2,1)} %copy-done) | copy-start | bytes 983044
  218.2 32.7 %copy-start.3 = (bf16[2048,80]{1,0:T(8,128)(2,1)S(1)}, bf16[2048,80]{1,0:T(8,128)(2,1)}, u32[]{:S(2)}) copy-start(bf16[2048,80]{1,0:T(8,128)(2,1)} %copy-done.2) | copy-start | bytes 983044
  224.8 32.7 %copy-start.5 = (bf16[2048,80]{1,0:T(8,128)(2,1)S(1)}, bf16[2048,80]{1,0:T(8,128)(2,1)}, u32[]{:S(2)}) copy-start(bf16[2048,80]{1,0:T(8,128)(2,1)} %copy-done.4) | copy-start | bytes 983044
  231.3 32.7 %copy-start.7 = (bf16[2048,80]{1,0:T(8,128)(2,1)S(1)}, bf16[2048,80]{1,0:T(8,128)(2,1)}, u32[]{:S(2)}) copy-start(bf16[2048,80]{1,0:T(8,128)(2,1)} %copy-done.6) | copy-start | bytes 983044
  237.8 32.6 %copy-start.9 = (bf16[2048,80]{1,0:T(8,128)(2,1)S(1)}, bf16[2048,80]{1,0:T(8,128)(2,1)}, u32[]{:S(2)}) copy-start(bf16[2048,80]{1,0:T(8,128)(2,1)} %copy-done.8) | copy-start | bytes 983044
  244.4 32.6 %copy-start.11 = (bf16[2048,80]{1,0:T(8,128)(2,1)S(1)}, bf16[2048,80]{1,0:T(8,128)(2,1)}, u32[]{:S(2)}) copy-start(bf16[2048,80]{1,0:T(8,128)(2,1)} %copy-done.10) | copy-start | bytes 983044
Sparse Core Ops, SparseCore 0:
  63.1 29.0 all-gather.1
  319.5 95.9 all-reduce.1
